TPU v7x, 32 devices: a whole 2x2x4 slice. The times are simulated.
32 devices in a mesh: req: 8 (over z, y), tp: 4 (over x, core).
Axes of the slice: x: 2, y: 2, z: 4, core: 2. Of those that a mesh axis runs over, the one named last changes fastest.
Arguments:
- tokens: bfloat16 [16384, 8192], P('req', 'tp'), may hold values from -6 to 6
- base_projection_weight: bfloat16 [8192, 2048], P('tp'), may hold values from -0.0625 to 0.0625
- adapter_down_maps: bfloat16 [128, 8192, 128], P('req', 'tp'), may hold values from -0.0625 to 0.0625
- adapter_up_maps: bfloat16 [128, 64, 2048], P('req', None, 'tp'), may hold values from -0.75 to 0.75
- block_adapter_ids: int32 [128], replicated, may hold values from 0 to 128, as said below
- adapter_storage_entry: int32 [128], replicated, may hold values from 0 to 127, as said below
Outputs:
- key_value: bfloat16 [16384, 2048], P('req', 'tp')
Inputs may be any that keep to these rules, and one draw needn't show every extreme that they name: `block_adapter_ids`: ids are 0 (base model) or 1 to 128. Adapter k is held by req index adapter_storage_entry[k - 1] // 16. Among the 16 blocks of one req index (blocks i * 16 to i * 16 + 15) at most 2 name adapters held by any one req index; in every draw one req index receives exactly 2 blocks, all naming one adapter, from every req index. `adapter_storage_entry`: A permutation: each storage entry holds exactly one adapter.
All inputs are finite; a program needn't handle non-finite values.
Results may differ from a plain program's by a relative error of at most 0.014.
Values may be sent and summed in bfloat16 or wider, within the bound.
A program may use at most 128 MiB of HBM per device.

v0:
```python
import jax
import jax.numpy as jnp
from jax import lax
from jax.sharding import PartitionSpec as P

KEY_WIDTH = 1024
BLOCK = 128
CAP = 2


def per_device(
    tokens,
    base_projection_weight,
    adapter_down_maps,
    adapter_up_maps,
    block_adapter_ids,
    adapter_storage_entry,
):
    req_count = lax.axis_size("req")
    my_req = lax.axis_index("req")
    my_tp = lax.axis_index("tp")
    row_count, feat_count = tokens.shape
    blk_count = row_count // BLOCK
    adapter_count = adapter_down_maps.shape[0]
    rank_width = adapter_up_maps.shape[1]
    column_count = adapter_up_maps.shape[2]
    half_index = my_tp * column_count // KEY_WIDTH
    tok_blocks = tokens.reshape(blk_count, BLOCK, feat_count)
    partial_value = jnp.dot(tokens, base_projection_weight, preferred_element_type=jnp.float32)
    base_sum = lax.psum_scatter(
        partial_value.astype(jnp.bfloat16), "tp", scatter_dimension=1, tiled=True
    ).astype(jnp.float32)
    ids_all = block_adapter_ids.reshape(req_count, blk_count)
    stored = adapter_storage_entry[jnp.maximum(ids_all - 1, 0)]
    owner_all = jnp.where(ids_all > 0, stored // adapter_count, -1)
    local_all = stored % adapter_count
    block_pos = jnp.arange(blk_count, dtype=jnp.int32)
    before = block_pos[None, :] < block_pos[:, None]
    same_owner = owner_all[:, :, None] == owner_all[:, None, :]
    slot_all = jnp.sum(same_owner & before[None], axis=2)
    ids_own = lax.dynamic_index_in_dim(ids_all, my_req, 0, keepdims=False)
    owner_own = lax.dynamic_index_in_dim(owner_all, my_req, 0, keepdims=False)
    slot_own = lax.dynamic_index_in_dim(slot_all, my_req, 0, keepdims=False)
    spot_index = jnp.maximum(owner_own, 0) * CAP + slot_own
    owner_ids = jnp.arange(req_count, dtype=jnp.int32)[:, None, None]
    slot_ids = jnp.arange(CAP, dtype=jnp.int32)[None, :, None]
    incoming = (owner_all[:, None, :] == my_req) & (slot_all[:, None, :] == slot_ids)
    in_valid = jnp.any(incoming, axis=2)
    input_resident = jnp.sum(jnp.where(incoming, local_all[:, None, :], 0), axis=2)
    outgoing = (owner_own[None, None, :] == owner_ids) & (slot_own[None, None, :] == slot_ids)
    out_valid = jnp.any(outgoing, axis=2)
    pick_block = jnp.sum(jnp.where(outgoing, block_pos[None, None, :], 0), axis=2)
    send_rows = jnp.where(
        out_valid[:, :, None, None], tok_blocks[pick_block], jnp.zeros((), tokens.dtype)
    )
    landed_rows = lax.all_to_all(send_rows, "req", split_axis=0, concat_axis=0, tiled=True)
    partial_shrink = jnp.einsum(
        "vhyf,vhfp->vhyp",
        landed_rows,
        adapter_down_maps[input_resident],
        preferred_element_type=jnp.float32,
    )
    down_projected = lax.psum(partial_shrink.astype(jnp.bfloat16), "tp")
    down_projected_half = lax.dynamic_slice_in_dim(
        down_projected, half_index * rank_width, rank_width, 3
    )
    adapter_delta = jnp.einsum(
        "zflj,zfjb->zflb",
        down_projected_half,
        adapter_up_maps[input_resident],
        preferred_element_type=jnp.float32,
    ).astype(jnp.bfloat16)
    adapter_delta = jnp.where(
        in_valid[:, :, None, None], adapter_delta, jnp.zeros((), jnp.bfloat16)
    )
    returned = lax.all_to_all(adapter_delta, "req", split_axis=0, concat_axis=0, tiled=True)
    own_delta = returned.reshape(req_count * CAP, BLOCK, column_count)[spot_index]
    own_delta = jnp.where(ids_own[:, None, None] > 0, own_delta, jnp.zeros((), jnp.bfloat16))
    return (base_sum + own_delta.reshape(row_count, column_count).astype(jnp.float32)).astype(
        jnp.bfloat16
    )


def solution(mesh):
    placed = (P("req", "tp"), P("tp", None), P("req", "tp", None), P("req", None, "tp"), P(), P())
    return jax.shard_map(
        per_device, mesh=mesh, in_specs=placed, out_specs=P("req", "tp"), check_vma=False
    )
```

profile of v0, /device:TPU:0, one launch (start us, length us, event | category | flops | bytes accessed | tf_op | source)
XLA Modules:
  0.0 343.1 jit_solution(5026651904690158362)
XLA Ops:
  6.5 0.0 copy-start
  6.5 0.7 add_maximum_fusion
  7.3 0.7 reshape.232
  8.0 1.6 gather_fusion
  9.6 0.1 reshape.236
  9.7 0.3 convert_reduce_fusion
  10.1 0.1 fusion.1
  10.2 0.2 and_reduce_fusion
  10.4 0.2 select_reduce_fusion
  10.6 0.1 copy.13
  10.6 0.1 reshape.245
  10.7 0.1 copy.12
  10.8 8.1 %gather_fusion.1 = bf16[16,128,2048]{2,1,0:T(8,128)(2,1)} fusion(bf16[16,128,2048]{2,1,0:T(8,128)(2,1)} %bitcast.36, s32[1024]{0:T(1024)S(1)} %pad_clamp_fusion.2), kind=kCustom, calls=%fused_computation.1 | custom fusion | bytes 16777280 | tf_op jit(solution)/shard_map/gather | solution.py:54
  19.0 7.2 %broadcast_select_fusion = bf16[8,2,128,2048]{3,2,1,0:T(8,128)(2,1)} fusion(bf16[8,2,128,2048]{3,2,1,0:T(8,128)(2,1)} %bitcast.35, pred[8,2]{1,0:T(8,128)(4,1)S(1)} %copy.12), kind=kLoop, calls=%fused_computation.5 | loop fusion | flops 4194304 | bytes 16777232 | tf_op jit(solution)/shard_map/jit(_where)/select_n | solution.py:53
  26.2 7.3 %all-to-all-start = ((bf16[8,2,128,2048]{3,2,1,0:T(8,128)(2,1)}), bf16[8,2,128,2048]{3,2,1,0:T(8,128)(2,1)}, u32[]{:S(2)}, u32[]{:S(2)}) async-start(bf16[8,2,128,2048]{3,2,1,0:T(8,128)(2,1)} %broadcast_select_fusion), calls=%async_computation.1 | async-start | bytes 16777216 | tf_op jit(solution)/shard_map/all_to_all | solution.py:56
  33.5 0.0 all-reduce.2.cloned.1.call-start
  33.5 0.1 copy.14
  33.6 0.1 reshape.253
  33.7 8.1 %gather_fusion.2 = bf16[16,2048,128]{2,1,0:T(8,128)(2,1)} fusion(bf16[16,2048,128]{2,1,0:T(8,128)(2,1)} %param.8, s32[1024]{0:T(1024)S(1)} %pad_clamp_fusion.1), kind=kCustom, calls=%fused_computation.2 | custom fusion | bytes 16777280 | tf_op jit(solution)/shard_map/gather | solution.py:60
  41.8 174.8 %all-to-all-done = bf16[8,2,128,2048]{3,2,1,0:T(8,128)(2,1)} async-done(((bf16[8,2,128,2048]{3,2,1,0:T(8,128)(2,1)}), bf16[8,2,128,2048]{3,2,1,0:T(8,128)(2,1)}, u32[]{:S(2)}, u32[]{:S(2)}) %all-to-all-start) | async-done | bytes 8388640 | tf_op jit(solution)/shard_map/all_to_all | solution.py:56
  216.6 9.4 %convolution_convert_fusion.1 = bf16[8,2,128,128]{2,3,1,0:T(8,128)(2,1)} fusion(bf16[8,2,128,2048]{3,2,1,0:T(8,128)(2,1)} %all-to-all-done, bf16[8,2,2048,128]{3,2,1,0:T(8,128)(2,1)} %bitcast.34), kind=kOutput, calls=%fused_computation.10 | convolution fusion | flops 1074003968 | bytes 17301504 | tf_op jit(solution)/shard_map/vhyf,vhfp->vhyp/dot_general | solution.py:57
  226.0 0.0 all-reduce.2.cloned.1.call-update
  226.0 0.0 reduce-scatter.2.cloned.1.call-start
  226.1 23.6 %convolution_convert_fusion = bf16[2048,2048]{1,0:T(8,128)(2,1)} fusion(bf16[2048,2048]{1,0:T(8,128)(2,1)} %param.6, bf16[2048,2048]{1,0:T(8,128)(2,1)} %param.7), kind=kOutput, calls=%fused_computation.6 | convolution fusion | flops 17184063488 | bytes 25165824 | tf_op jit(solution)/shard_map/dot_general | solution.py:29
  249.6 0.0 reduce-scatter.2.cloned.1.call-update
  249.7 0.0 copy-done
  249.7 0.6 gather_fusion.3
  250.3 0.1 fusion.3
  250.5 0.1 copy.11
  250.6 7.8 %all-reduce.2.cloned.1.call-done = bf16[8,2,128,128]{2,3,1,0:T(8,128)(2,1)} async-done(((bf16[8,2,128,128]{2,3,1,0:T(8,128)(2,1)}), bf16[8,2,128,128]{2,3,1,0:T(8,128)(2,1)}) %all-reduce.2.cloned.1.call-update) | async-done | bytes 524304 | tf_op jit(solution)/shard_map/psum | solution.py:63
  258.4 3.1 convert_select_fusion
  261.5 5.5 %all-to-all-start.1 = ((bf16[8,2,128,512]{3,2,1,0:T(8,128)(2,1)}), bf16[8,2,128,512]{3,2,1,0:T(8,128)(2,1)S(1)}, u32[]{:S(2)}, u32[]{:S(2)}) async-start(bf16[8,2,128,512]{3,2,1,0:T(8,128)(2,1)} %convert_select_fusion), calls=%async_computation.2 | async-start | bytes 4194304 | tf_op jit(solution)/shard_map/all_to_all | solution.py:76
  267.1 0.1 broadcast_bitcast_fusion
  267.1 47.2 %all-to-all-done.1 = bf16[8,2,128,512]{3,2,1,0:T(8,128)(2,1)S(1)} async-done(((bf16[8,2,128,512]{3,2,1,0:T(8,128)(2,1)}), bf16[8,2,128,512]{3,2,1,0:T(8,128)(2,1)S(1)}, u32[]{:S(2)}, u32[]{:S(2)}) %all-to-all-start.1) | async-done | bytes 2097184 | tf_op jit(solution)/shard_map/all_to_all | solution.py:76
  314.3 2.0 gather_fusion.4
  316.3 16.4 %reduce-scatter.2.cloned.1.call-done = bf16[2048,512]{1,0:T(8,128)(2,1)} async-done(((bf16[2048,2048]{1,0:T(8,128)(2,1)}), bf16[2048,512]{1,0:T(8,128)(2,1)}) %reduce-scatter.2.cloned.1.call-update) | async-done | bytes 2097168 | tf_op jit(solution)/shard_map/reduce_scatter | solution.py:30
  332.7 3.5 %add_convert_fusion = bf16[2048,512]{1,0:T(8,128)(2,1)} fusion(bf16[2048,512]{1,0:T(8,128)(2,1)} %reduce-scatter.2.cloned.1.call-done, bf16[16,128,512]{2,1,0:T(8,128)(2,1)} %gather_fusion.4, pred[2048]{0:T(1024)(128)(4,1)S(1)} %broadcast_bitcast_fusion), kind=kLoop, calls=%fused_computation.7 | loop fusion | flops 5242880 | bytes 6293504 | tf_op jit(solution)/shard_map/convert_element_type | solution.py:79
  (14 shorter events, 0.1 us)
Async XLA Ops:
  6.5 243.2 %copy-start = (bf16[16,64,512]{2,1,0:T(8,128)(2,1)S(1)}, bf16[16,64,512]{2,1,0:T(8,128)(2,1)}, u32[]{:S(2)}) copy-start(bf16[16,64,512]{2,1,0:T(8,128)(2,1)} %param.9) | copy-start | bytes 3145732
  26.2 190.4 %all-to-all-start = ((bf16[8,2,128,2048]{3,2,1,0:T(8,128)(2,1)}), bf16[8,2,128,2048]{3,2,1,0:T(8,128)(2,1)}, u32[]{:S(2)}, u32[]{:S(2)}) async-start(bf16[8,2,128,2048]{3,2,1,0:T(8,128)(2,1)} %broadcast_select_fusion), calls=%async_computation.1 | async-start | bytes 16777216 | tf_op jit(solution)/shard_map/all_to_all | solution.py:56
  33.5 224.9 %all-reduce.2.cloned.1.call-start = ((), (), s32[]{:S(2)}) async-start(), calls=%async_computation.4 | async-start | bytes 1048576 | tf_op jit(solution)/shard_map/psum | solution.py:63
  226.0 106.7 %reduce-scatter.2.cloned.1.call-start = ((), (), s32[]{:S(2)}) async-start(), calls=%async_computation.3 | async-start | bytes 10485760 | tf_op jit(solution)/shard_map/reduce_scatter | solution.py:30
  261.5 52.8 %all-to-all-start.1 = ((bf16[8,2,128,512]{3,2,1,0:T(8,128)(2,1)}), bf16[8,2,128,512]{3,2,1,0:T(8,128)(2,1)S(1)}, u32[]{:S(2)}, u32[]{:S(2)}) async-start(bf16[8,2,128,512]{3,2,1,0:T(8,128)(2,1)} %convert_select_fusion), calls=%async_computation.2 | async-start | bytes 4194304 | tf_op jit(solution)/shard_map/all_to_all | solution.py:76
Sparse Core Ops, SparseCore 0:
  226.1 32.2 all-reduce.1
  261.0 71.7 reduce-scatter.1
where the time goes:
time: 344 us; the launch traced here: 343 us
  waiting for transfers between devices  246 us (72%)
  matrix products  36 us (10%)
  local copies, waits for them, and re-layouts  21.9 us (6%)
  between operations  13.5 us (4%)
  starting transfers between devices  12.9 us (4%)
  other arithmetic  12.5 us (4%)
    all_to_all x1, waiting for transfers between devices, per_device(): lax.all_to_all(send_rows, 'req', split_axis=0, concat_axis=0, tiled=True)  175 us
    all_to_all x1, waiting for transfers between devices, per_device(): lax.all_to_all(adapter_delta, 'req', split_axis=0, concat_axis=0, tiled=T...  47.2 us
    dot_general x1, matrix products, per_device(): jnp.dot(tokens, base_projection_weight, preferred_element_type=jnp.float32)  23.6 us
    reduce_scatter x1, waiting for transfers between devices, per_device(): lax.psum_scatter(partial_value.astype(jnp.bfloat16), 'tp', scatter_dimens...  16.4 us
    dot_general x1, matrix products, per_device(): jnp.einsum('vhyf,vhfp->vhyp', landed_rows, adapter_down_maps[input_reside...  9.37 us
    gather x1, local copies, waits for them, and re-layouts, per_device(): adapter_down_maps[input_resident]  8.15 us
    gather x1, local copies, waits for them, and re-layouts, per_device(): tok_blocks[pick_block]  8.14 us
    psum x1, waiting for transfers between devices, per_device(): down_projected = lax.psum(partial_shrink.astype(jnp.bfloat16), 'tp')  7.84 us
  transfers between devices with their start and end apart: 4, of which 4 were waited for; matrix products, arithmetic and copies ran while one was open for 11% of the time, Pallas kernels for 0%

commit v1 on v0

--- a/solution.py
+++ b/solution.py
@@ -60,7 +60,7 @@
         adapter_down_maps[input_resident],
         preferred_element_type=jnp.float32,
     )
-    down_projected = lax.psum(partial_shrink.astype(jnp.bfloat16), "tp")
+    down_projected = jnp.sum(lax.all_gather(partial_shrink.astype(jnp.bfloat16), "tp"), axis=0)
     down_projected_half = lax.dynamic_slice_in_dim(
         down_projected, half_index * rank_width, rank_width, 3
     )

time: 344 us -> 333 us (0.968)
  waiting for transfers between devices: 246 us -> 237 us
    psum x1 -> x0, waiting for transfers between devices: 7.84 us -> none  [per_device(): down_projected = lax.psum(partial_shrink.astype(jnp.bfloat16), 'tp')]
  transfers between devices with their start and end apart: 4 -> 4, of which waited for: 4 -> 3; matrix products, arithmetic and copies ran while one was open for 11% -> 12% of each run, Pallas kernels for 0% -> 0%
where the time goes in v1:
time: 333 us; the launch traced here: 332 us
  waiting for transfers between devices  237 us (71%)
  matrix products  34.5 us (10%)
  local copies, waits for them, and re-layouts  21.9 us (7%)
  other arithmetic  14.5 us (4%)
  between operations  13.6 us (4%)
  starting transfers between devices  11 us (3%)
    all_to_all x1, waiting for transfers between devices, per_device(): lax.all_to_all(send_rows, 'req', split_axis=0, concat_axis=0, tiled=True)  175 us
    all_to_all x1, waiting for transfers between devices, per_device(): lax.all_to_all(adapter_delta, 'req', split_axis=0, concat_axis=0, tiled=T...  48.3 us
    dot_general x1, matrix products, per_device(): jnp.dot(tokens, base_projection_weight, preferred_element_type=jnp.float32)  23.6 us
    reduce_scatter x1, waiting for transfers between devices, per_device(): lax.psum_scatter(partial_value.astype(jnp.bfloat16), 'tp', scatter_dimens...  13.5 us
    dot_general x1, matrix products, per_device(): jnp.einsum('vhyf,vhfp->vhyp', landed_rows, adapter_down_maps[input_reside...  8.9 us
    gather x1, local copies, waits for them, and re-layouts, per_device(): adapter_down_maps[input_resident]  8.15 us
    gather x1, local copies, waits for them, and re-layouts, per_device(): tok_blocks[pick_block]  8.14 us
    all_to_all x1, starting transfers between devices, per_device(): lax.all_to_all(send_rows, 'req', split_axis=0, concat_axis=0, tiled=True)  7.28 us
  transfers between devices with their start and end apart: 4, of which 3 were waited for; matrix products, arithmetic and copies ran while one was open for 12% of the time, Pallas kernels for 0%

profile of v1, /device:TPU:0, one launch (start us, length us, event | category | flops | bytes accessed | tf_op | source)
XLA Modules:
  0.0 332.1 jit_solution(6182144362621266793)
XLA Ops:
  6.5 0.0 copy-start
  6.5 0.7 add_maximum_fusion
  7.3 0.7 reshape.232
  8.0 1.6 gather_fusion
  9.6 0.1 reshape.236
  9.7 0.3 convert_reduce_fusion
  10.1 0.1 fusion.1
  10.2 0.2 and_reduce_fusion
  10.4 0.2 select_reduce_fusion
  10.6 0.1 copy.16
  10.6 0.1 reshape.245
  10.7 0.1 copy.15
  10.8 8.1 %gather_fusion.1 = bf16[16,128,2048]{2,1,0:T(8,128)(2,1)} fusion(bf16[16,128,2048]{2,1,0:T(8,128)(2,1)} %bitcast.37, s32[1024]{0:T(1024)S(1)} %pad_clamp_fusion.2), kind=kCustom, calls=%fused_computation.1 | custom fusion | bytes 16777280 | tf_op jit(solution)/shard_map/gather | solution.py:54
  19.0 7.2 %broadcast_select_fusion = bf16[8,2,128,2048]{3,2,1,0:T(8,128)(2,1)} fusion(bf16[8,2,128,2048]{3,2,1,0:T(8,128)(2,1)} %bitcast.36, pred[8,2]{1,0:T(8,128)(4,1)S(1)} %copy.15), kind=kLoop, calls=%fused_computation.5 | loop fusion | flops 4194304 | bytes 16777232 | tf_op jit(solution)/shard_map/jit(_where)/select_n | solution.py:53
  26.2 7.3 %all-to-all-start = ((bf16[8,2,128,2048]{3,2,1,0:T(8,128)(2,1)}), bf16[8,2,128,2048]{3,2,1,0:T(8,128)(2,1)}, u32[]{:S(2)}, u32[]{:S(2)}) async-start(bf16[8,2,128,2048]{3,2,1,0:T(8,128)(2,1)} %broadcast_select_fusion), calls=%async_computation.1 | async-start | bytes 16777216 | tf_op jit(solution)/shard_map/all_to_all | solution.py:56
  33.5 0.0 all-gather.3.cloned.1.call-start
  33.5 0.1 copy.17
  33.6 0.1 reshape.253
  33.7 8.1 %gather_fusion.2 = bf16[16,2048,128]{2,1,0:T(8,128)(2,1)} fusion(bf16[16,2048,128]{2,1,0:T(8,128)(2,1)} %param.8, s32[1024]{0:T(1024)S(1)} %pad_clamp_fusion.1), kind=kCustom, calls=%fused_computation.2 | custom fusion | bytes 16777280 | tf_op jit(solution)/shard_map/gather | solution.py:60
  41.8 174.8 %all-to-all-done = bf16[8,2,128,2048]{3,2,1,0:T(8,128)(2,1)} async-done(((bf16[8,2,128,2048]{3,2,1,0:T(8,128)(2,1)}), bf16[8,2,128,2048]{3,2,1,0:T(8,128)(2,1)}, u32[]{:S(2)}, u32[]{:S(2)}) %all-to-all-start) | async-done | bytes 8388640 | tf_op jit(solution)/shard_map/all_to_all | solution.py:56
  216.6 8.9 %convolution_convert_fusion.1 = bf16[8,2,128,128]{3,2,1,0:T(8,128)(2,1)} fusion(bf16[8,2,128,2048]{3,2,1,0:T(8,128)(2,1)} %all-to-all-done, bf16[8,2,2048,128]{3,2,1,0:T(8,128)(2,1)} %bitcast.35), kind=kOutput, calls=%fused_computation.10 | convolution fusion | flops 1074003968 | bytes 17301504 | tf_op jit(solution)/shard_map/vhyf,vhfp->vhyp/dot_general | solution.py:57
  225.5 0.0 all-gather.3.cloned.1.call-update
  225.6 0.0 reduce-scatter.2.cloned.1.call-start
  225.6 23.6 %convolution_convert_fusion = bf16[2048,2048]{1,0:T(8,128)(2,1)} fusion(bf16[2048,2048]{1,0:T(8,128)(2,1)} %param.6, bf16[2048,2048]{1,0:T(8,128)(2,1)} %param.7), kind=kOutput, calls=%fused_computation.6 | convolution fusion | flops 17184063488 | bytes 25165824 | tf_op jit(solution)/shard_map/dot_general | solution.py:29
  249.2 0.0 reduce-scatter.2.cloned.1.call-update
  249.2 0.0 copy-done
  249.2 0.6 gather_fusion.3
  249.8 0.1 fusion.3
  250.0 0.1 copy.14
  250.1 0.0 all-gather.3.cloned.1.call-done
  250.1 2.0 reduce_sum.48
  252.1 2.1 convert_select_fusion
  254.2 3.6 %all-to-all-start.1 = ((bf16[8,2,128,512]{3,2,1,0:T(8,128)(2,1)}), bf16[8,2,128,512]{3,2,1,0:T(8,128)(2,1)S(1)}, u32[]{:S(2)}, u32[]{:S(2)}) async-start(bf16[8,2,128,512]{3,2,1,0:T(8,128)(2,1)} %convert_select_fusion), calls=%async_computation.2 | async-start | bytes 4194304 | tf_op jit(solution)/shard_map/all_to_all | solution.py:76
  257.9 0.1 broadcast_bitcast_fusion
  258.0 48.3 %all-to-all-done.1 = bf16[8,2,128,512]{3,2,1,0:T(8,128)(2,1)S(1)} async-done(((bf16[8,2,128,512]{3,2,1,0:T(8,128)(2,1)}), bf16[8,2,128,512]{3,2,1,0:T(8,128)(2,1)S(1)}, u32[]{:S(2)}, u32[]{:S(2)}) %all-to-all-start.1) | async-done | bytes 2097184 | tf_op jit(solution)/shard_map/all_to_all | solution.py:76
  306.3 2.0 gather_fusion.4
  308.2 13.5 %reduce-scatter.2.cloned.1.call-done = bf16[2048,512]{1,0:T(8,128)(2,1)} async-done(((bf16[2048,2048]{1,0:T(8,128)(2,1)}), bf16[2048,512]{1,0:T(8,128)(2,1)}) %reduce-scatter.2.cloned.1.call-update) | async-done | bytes 2097168 | tf_op jit(solution)/shard_map/reduce_scatter | solution.py:30
  321.7 3.5 %add_convert_fusion = bf16[2048,512]{1,0:T(8,128)(2,1)} fusion(bf16[2048,512]{1,0:T(8,128)(2,1)} %reduce-scatter.2.cloned.1.call-done, bf16[16,128,512]{2,1,0:T(8,128)(2,1)} %gather_fusion.4, pred[2048]{0:T(1024)(128)(4,1)S(1)} %broadcast_bitcast_fusion), kind=kLoop, calls=%fused_computation.7 | loop fusion | flops 5242880 | bytes 6293504 | tf_op jit(solution)/shard_map/convert_element_type | solution.py:79
  (14 shorter events, 0.1 us)
Async XLA Ops:
  6.5 242.7 %copy-start = (bf16[16,64,512]{2,1,0:T(8,128)(2,1)S(1)}, bf16[16,64,512]{2,1,0:T(8,128)(2,1)}, u32[]{:S(2)}) copy-start(bf16[16,64,512]{2,1,0:T(8,128)(2,1)} %param.9) | copy-start | bytes 3145732
  26.2 190.4 %all-to-all-start = ((bf16[8,2,128,2048]{3,2,1,0:T(8,128)(2,1)}), bf16[8,2,128,2048]{3,2,1,0:T(8,128)(2,1)}, u32[]{:S(2)}, u32[]{:S(2)}) async-start(bf16[8,2,128,2048]{3,2,1,0:T(8,128)(2,1)} %broadcast_select_fusion), calls=%async_computation.1 | async-start | bytes 16777216 | tf_op jit(solution)/shard_map/all_to_all | solution.py:56
  33.5 216.6 %all-gather.3.cloned.1.call-start = ((), (), s32[]{:S(2)}) async-start(), calls=%async_computation.4 | async-start | bytes 2621440 | tf_op jit(solution)/shard_map/all_gather | solution.py:63
  225.6 96.2 %reduce-scatter.2.cloned.1.call-start = ((), (), s32[]{:S(2)}) async-start(), calls=%async_computation.3 | async-start | bytes 10485760 | tf_op jit(solution)/shard_map/reduce_scatter | solution.py:30
  254.2 52.1 %all-to-all-start.1 = ((bf16[8,2,128,512]{3,2,1,0:T(8,128)(2,1)}), bf16[8,2,128,512]{3,2,1,0:T(8,128)(2,1)S(1)}, u32[]{:S(2)}, u32[]{:S(2)}) async-start(bf16[8,2,128,512]{3,2,1,0:T(8,128)(2,1)} %convert_select_fusion), calls=%async_computation.2 | async-start | bytes 4194304 | tf_op jit(solution)/shard_map/all_to_all | solution.py:76
Sparse Core Ops, SparseCore 0:
  225.7 21.6 all-gather.2
  249.9 71.7 reduce-scatter.1
